TPU v7x, 32 devices: a whole 2x2x4 slice. The times are simulated.
32 devices in a mesh: chan: 4 (over y, core), tile: 8 (over z, x).
Axes of the slice: x: 2, y: 2, z: 4, core: 2. Of those that a mesh axis runs over, the one named last changes fastest.
Arguments:
- dirty: float32 [2, 36, 128, 128], P(None, 'chan', 'tile'), may hold values from -6 to 6
- beams: float32 [36, 289], P('chan'), may hold values from -0.24 to 0.24
- chan_bins: int32 [36], replicated, may hold values from 0 to 287
- pixel_order: int32 [8, 2048], P('tile'), may hold values from 0 to 2047, each once within a row
Outputs:
- spectrum: float32 [2, 256, 8, 2048], P(None, None, 'tile', 'chan')
- residual: float32 [2, 36, 128, 128], P(None, 'chan', 'tile')
Inputs may be any that keep to these rules, and one draw needn't show every extreme that they name: `pixel_order`: each row is a permutation of 0 to 2047.
All inputs are finite; a program needn't handle non-finite values.
Results may differ from a plain program's by a relative error of at most 0.000068.
Values sent between devices are 32-bit elements; how exact they have to be, the bound alone decides.
A program may use at most 64 MiB of HBM per device.

v0:
```python
import functools
import math

import jax
import jax.numpy as jnp
from jax import lax
from jax.experimental import pallas as pl
from jax.experimental.pallas import tpu as pltpu
from jax.sharding import PartitionSpec as P

DEPTHS = 256
BINS = 288
THRESHOLD = 0.8
STEP_SIZE = 0.5
MESH = pl.DeviceIdType.MESH
LANES = 128
F32 = jnp.float32
BF16 = jnp.bfloat16


def round_up(value, unit):
    return (value + unit - 1) // unit * unit


def split(x):
    high = x.astype(BF16)
    return high, (x - high.astype(F32)).astype(BF16)


def shrink_pair(a, b):
    squared = a * a + b * b
    factor = jnp.maximum(1.0 - THRESHOLD * lax.rsqrt(jnp.maximum(squared, 1e-30)), 0.0)
    return a * factor, b * factor


def aligned(row):
    return row if isinstance(row, int) else pl.multiple_of(row, 8)


def mxu(a, b):
    return jnp.dot(a, b, preferred_element_type=F32)


def kernel(
    d,
    dirty_hbm,
    beams_hbm,
    bins_hbm,
    order_hbm,
    big,
    first_slots,
    res,
    dirty,
    beams,
    bins,
    order,
    bincol,
    at3,
    a3,
    at2,
    x,
    first_hi,
    first_lo,
    model,
    padded,
    slots,
    mixed,
    send_a,
    send_d,
    send_m,
    send_r,
    recv_a,
    recv_d,
    recv_m,
    recv_h,
    recv_r,
    sems_a,
    sems_d,
    sems_m,
    sems_h,
    sems_r,
    sems_in,
):
    G, T, R, Y, C, S, W, CC, NCH, HALF, BEAM = (
        d["G"], d["T"], d["R"], d["Y"], d["C"], d["S"], d["W"], d["CC"], d["NCH"], d["HALF"], d["BEAM"]
    )
    SC = S * C
    KP = d["KP"]
    g = lax.axis_index("chan")
    t = lax.axis_index("tile")
    has_prev = t > 0
    has_next = t < T - 1
    before = lax.rem(t + T - 1, T)
    after = lax.rem(t + 1, T)

    pairs = ((dirty_hbm, dirty), (bins_hbm, bins), (beams_hbm, beams), (order_hbm, order))
    loads = [pltpu.make_async_copy(src, dst, sems_in.at[n]) for n, (src, dst) in enumerate(pairs)]
    for load in loads:
        load.start()
    barrier = pltpu.get_barrier_semaphore()
    for step in range(1, G):
        pl.semaphore_signal(barrier, inc=1, device_id=(lax.rem(g + step, G), t), device_id_type=MESH)

    @pl.when(has_prev)
    def _():
        for p in range(G):
            pl.semaphore_signal(barrier, inc=1, device_id=(p, before), device_id_type=MESH)

    @pl.when(has_next)
    def _():
        for p in range(G):
            pl.semaphore_signal(barrier, inc=1, device_id=(p, after), device_id_type=MESH)

    def pack(send, k, cells):
        for p in range(G):
            for r in range(R):
                send[p, k, r * W : r * W + W, :] = cells[pl.ds(k * W * Y + p * R + r, W, stride=Y), :]

    loads[0].wait()
    for c in range(C):
        for s in range(S):
            mixed[(c * S + s) * Y : (c * S + s) * Y + Y, :] = dirty[(s * C + c) * Y : (s * C + c) * Y + Y, :]
    for k in range(NCH):
        pack(send_a, k, mixed)
    near = has_prev.astype(jnp.int32) + has_next.astype(jnp.int32)
    pl.semaphore_wait(barrier, G - 1 + G * near)

    def own_copies(src, dst, sems, *k):
        out_copies, in_copies = [], []
        for step in range(1, G):
            p = lax.rem(g + step, G)
            out_copies.append(
                pltpu.make_async_remote_copy(
                    src(p), dst(g), sems.at[(0, p, *k)], sems.at[(1, g, *k)], device_id=(p, t), device_id_type=MESH
                )
            )
            in_copies.append(
                pltpu.make_async_remote_copy(
                    src(p), dst(p), sems.at[(0, p, *k)], sems.at[(1, p, *k)], device_id=(p, t), device_id_type=MESH
                )
            )
        return out_copies, in_copies

    out_a, in_a = own_copies(lambda p: send_a.at[p], lambda p: recv_a.at[p], sems_a)
    for copy in out_a:
        copy.start()
    recv_a[g] = send_a[g]

    for load in loads[1:]:
        load.wait()
    bincol[...] = jnp.zeros_like(bincol)
    for row in range(G * C):
        bincol[S * row : S * row + S, :] = jnp.full((S, LANES), bins[row].astype(F32))
    scale = 1.0 / math.sqrt(G * C)
    at3[...] = jnp.zeros_like(at3)
    for piece in range(DEPTHS // LANES):
        shape = (KP, LANES)
        depth = lax.broadcasted_iota(jnp.int32, shape, 1) + (piece * LANES - DEPTHS // 2)
        product = bincol[...] * depth.astype(F32)
        turns = product - BINS * jnp.floor(product * (1.0 / BINS))
        turns = jnp.where(turns < 0, turns + BINS, turns)
        turns = jnp.where(turns >= BINS, turns - BINS, turns)
        angles = turns * (2.0 * math.pi / BINS)
        row = lax.broadcasted_iota(jnp.int32, shape, 0)
        is_q = (row & 1) == 0
        real = row < G * SC
        cosine = jnp.where(real, jnp.cos(angles) * scale, 0.0)
        sine = jnp.where(real, jnp.sin(angles) * scale, 0.0)
        for half, value in ((0, jnp.where(is_q, cosine, sine)), (1, jnp.where(is_q, -sine, cosine))):
            lanes = pl.ds(half * DEPTHS + piece * LANES, LANES)
            high, low = split(value)
            at2[0:KP, lanes] = high
            at2[KP : 2 * KP, lanes] = low
            at3[0:KP, lanes] = high.astype(F32)
            at3[KP : 2 * KP, lanes] = low.astype(F32)
            at3[2 * KP : 3 * KP, lanes] = high.astype(F32)
    a3[...] = at3[...].T.astype(BF16)
    x[...] = jnp.zeros_like(x)

    shift = int(math.log2(LANES))

    def permute(cells):
        halves = []
        for h in range(Y // 8):
            pixel = order[8 * h : 8 * h + 8, :]
            col = pixel & (LANES - 1)
            row = lax.shift_right_logical(pixel, shift)
            acc = jnp.zeros((8, LANES), F32)
            for y in range(Y):
                taken = jnp.take_along_axis(cells(y), col, axis=1, mode="promise_in_bounds")
                acc = jnp.where(row == y, taken, acc)
            halves.append(acc)
        return jnp.concatenate(halves, axis=0)

    def gather_dirty(c, carry):
        for s in range(S):
            source = (s * C + c) * Y
            target = pl.ds(aligned((c * S + s) * Y), Y)
            slots[target, :] = permute(lambda y: jnp.broadcast_to(dirty[pl.ds(source + y, 1), :], (8, LANES)))
        return carry

    def project(recv):
        for q in range(G):
            for k in range(NCH):
                for r in range(R):
                    x[q * SC + k * W : q * SC + k * W + W, r * LANES : (r + 1) * LANES] = recv[
                        q, k, r * W : r * W + W, :
                    ]
        high, low = split(x[...])
        parts = [high, high, low]
        if d["K3"] > 3 * KP:
            parts.append(jnp.zeros((d["K3"] - 3 * KP, x.shape[1]), BF16))
        big[...] = mxu(a3[...], jnp.concatenate(parts, axis=0))

    BLOCK = 16

    for copy in in_a:
        copy.wait_recv()
    project(recv_a)

    def shrink_first(i, carry):
        top = pl.ds(pl.multiple_of(i * BLOCK, BLOCK), BLOCK)
        low = pl.ds(pl.multiple_of(DEPTHS + i * BLOCK, BLOCK), BLOCK)
        a, b = shrink_pair(big[top, :], big[low, :])
        first_hi[top, :], first_lo[top, :] = split(a)
        first_hi[low, :], first_lo[low, :] = split(b)
        return carry

    lax.fori_loop(0, DEPTHS // BLOCK, shrink_first, 0)
    both = mxu(at2[...], first_hi[...])
    model[...] = both[:KP] + both[KP:] + mxu(at2[0:KP, :], first_lo[...])

    up = g * R < HALF
    goes = jnp.logical_or(jnp.logical_and(up, has_prev), jnp.logical_and(jnp.logical_not(up), has_next))
    toward = jnp.where(up, before, after)
    copies_m, copies_h = [], []
    for k in range(NCH):
        for p in range(G):
            for r in range(R):
                send_m[p, k, r * W : r * W + W, :] = model[
                    p * SC + k * W : p * SC + k * W + W, r * LANES : (r + 1) * LANES
                ]
        halo = [
            pltpu.make_async_remote_copy(
                send_m.at[p, k],
                recv_h.at[g, k],
                sems_h.at[0, p, k],
                sems_h.at[1, g, k],
                device_id=(p, toward),
                device_id_type=MESH,
            )
            for p in range(G)
        ]
        copies_h.append(halo)

        @pl.when(goes)
        def _():
            for copy in halo:
                copy.start()

        copies = own_copies(
            lambda p: send_m.at[p, k], lambda p: recv_m.at[p, k], sems_m, k
        )
        copies_m.append(copies)
        for copy in copies[0]:
            copy.start()
        recv_m[g, k] = send_m[g, k]

    lax.fori_loop(0, C, gather_dirty, 0)
    for k in range(NCH):
        pack(send_d, k, slots)
    out_d, in_d = own_copies(lambda p: send_d.at[p], lambda p: recv_d.at[p], sems_d)
    for copy in out_d:
        copy.start()
    recv_d[g] = send_d[g]

    PY = Y + 2 * HALF
    lane = lax.broadcasted_iota(jnp.int32, (Y, LANES), 1)
    blocks = [range(0, (BEAM + 1) // 2), range((BEAM + 1) // 2, BEAM)]

    def convolve(c, carry):
        totals = [jnp.zeros((Y, LANES), F32) for _ in range(S)]
        for block in blocks:
            sums = [[None] * len(block) for _ in range(S)]
            for i in range(BEAM):
                rows = [padded[pl.ds((c * S + s) * PY + i, Y), :] for s in range(S)]
                for n, j in enumerate(block):
                    tap = beams[c, i * BEAM + j]
                    for s in range(S):
                        term = tap * rows[s]
                        sums[s][n] = term if i == 0 else sums[s][n] + term
            for n, j in enumerate(block):
                inside = jnp.logical_and(lane + (j - HALF) >= 0, lane + (j - HALF) < LANES)
                for s in range(S):
                    moved = sums[s][n]
                    if j != HALF:
                        moved = pltpu.roll(moved, (HALF - j) % LANES, axis=1)
                        moved = jnp.where(inside, moved, 0.0)
                    totals[s] = totals[s] + moved
        for s in range(S):
            cells = pl.ds(aligned((s * C + c) * Y), Y)
            res[cells, :] = dirty[cells, :] - totals[s]
        return carry

    def gather_res(c, carry):
        for s in range(S):
            source = (s * C + c) * Y
            target = pl.ds(aligned((c * S + s) * Y), Y)
            slots[target, :] = permute(lambda y: jnp.broadcast_to(res[pl.ds(source + y, 1), :], (8, LANES)))
        return carry

    def halo_block(q, k, ok):
        arrived = pltpu.make_async_remote_copy(
            send_m.at[q, k],
            recv_h.at[q, k],
            sems_h.at[0, q, k],
            sems_h.at[1, q, k],
            device_id=(q, t),
            device_id_type=MESH,
        )

        @pl.when(ok)
        def _():
            arrived.wait_recv()

        @pl.when(jnp.logical_not(ok))
        def _():
            recv_h[q, k] = jnp.zeros(recv_h.shape[2:], F32)

    copies_r = []

    def step(c, carry):
        gather_res(c - 1, 0)
        return convolve(c, carry)

    def send_slots(k):
        pack(send_r, k, slots)
        copies = own_copies(lambda p: send_r.at[p, k], lambda p: recv_r.at[p, k], sems_r, k)
        copies_r.append(copies)
        for copy in copies[0]:
            copy.start()
        recv_r[g, k] = send_r[g, k]

    for k in range(NCH):
        for copy in copies_m[k][1]:
            copy.wait_recv()
        for q in range(G):
            from_next = q * R < HALF
            halo_block(q, k, has_next if from_next else has_prev)
            at_row = Y + HALF + q * R if from_next else q * R - HALF
            for r in range(R):
                padded[pl.ds(k * W * PY + HALF + q * R + r, W, stride=PY), :] = recv_m[
                    q, k, r * W : r * W + W, :
                ]
                padded[pl.ds(k * W * PY + at_row + r, W, stride=PY), :] = recv_h[
                    q, k, r * W : r * W + W, :
                ]
        if k == 0:
            convolve(0, 0)
        else:
            step(k * CC, 0)
            send_slots(k - 1)
        lax.fori_loop(k * CC + 1, (k + 1) * CC, step, 0)
    gather_res(C - 1, 0)
    send_slots(NCH - 1)

    for copy in in_d:
        copy.wait_recv()
    project(recv_d)

    def shrink_slots(i, carry):
        top = pl.ds(pl.multiple_of(i * BLOCK, BLOCK), BLOCK)
        low = pl.ds(pl.multiple_of(DEPTHS + i * BLOCK, BLOCK), BLOCK)
        first_slots[top, :], first_slots[low, :] = shrink_pair(big[top, :], big[low, :])
        return carry

    lax.fori_loop(0, DEPTHS // BLOCK, shrink_slots, 0)

    for k in range(NCH):
        for copy in copies_r[k][1]:
            copy.wait_recv()
    project(recv_r)

    for copy in out_a + out_d:
        copy.wait_send()
    for k in range(NCH):
        for copy in copies_m[k][0] + copies_r[k][0]:
            copy.wait_send()

    @pl.when(goes)
    def _():
        for halo in copies_h:
            for copy in halo:
                copy.wait_send()


PARTS = 4


def finish_kernel(R, update, first, cells, out, res, stage, sems):
    copies = [pltpu.make_async_copy(cells, res, sems.at[0])]
    copies[0].start()
    block = 16

    def shrink_second(i, carry):
        top = pl.ds(pl.multiple_of(i * block, block), block)
        low = pl.ds(pl.multiple_of(DEPTHS + i * block, block), block)
        a, b = shrink_pair(
            first[top, :] + STEP_SIZE * update[top, :], first[low, :] + STEP_SIZE * update[low, :]
        )
        for start, value in ((0, a), (DEPTHS, b)):
            for r in range(R):
                stage[pl.ds((start + i * block) * R + r, block, stride=R), :] = value[
                    :, r * LANES : (r + 1) * LANES
                ]
        return carry

    steps = DEPTHS // block // PARTS
    rows = DEPTHS * R // PARTS
    for part in range(PARTS):
        lax.fori_loop(part * steps, (part + 1) * steps, shrink_second, 0)
        for half in range(2):
            span = pl.ds(half * DEPTHS * R + part * rows, rows)
            copy = pltpu.make_async_copy(stage.at[span], out.at[span], sems.at[1 + 2 * part + half])
            copy.start()
            copies.append(copy)
    for copy in copies:
        copy.wait()


def on_device(dirty, beams, chan_bins, pixel_order):
    S, C, Y, X = dirty.shape
    G = lax.axis_size("chan")
    T = lax.axis_size("tile")
    BEAM = math.isqrt(beams.shape[1])
    HALF = (BEAM - 1) // 2
    R = Y // G
    CC = 3 if C % 3 == 0 else C
    NCH = C // CC
    W = S * CC
    SC = S * C
    KP = round_up(G * SC, 16)
    K3 = round_up(3 * KP, LANES)
    PB = round_up(R * W, 8)
    N = R * X
    d = dict(G=G, T=T, R=R, Y=Y, C=C, S=S, W=W, CC=CC, NCH=NCH, HALF=HALF, BEAM=BEAM, KP=KP, K3=K3)
    vmem = pl.BlockSpec(memory_space=pltpu.VMEM)
    hbm = pl.BlockSpec(memory_space=pltpu.HBM)
    block = pltpu.VMEM((G, NCH, PB, LANES), F32)
    dma = pltpu.SemaphoreType.DMA
    args = (dirty.reshape(SC * Y, X), beams, chan_bins, pixel_order.reshape(Y, X))
    update, first, cells = pl.pallas_call(
        functools.partial(kernel, d),
        out_shape=(
            jax.ShapeDtypeStruct((2 * DEPTHS, N), F32),
            jax.ShapeDtypeStruct((2 * DEPTHS, N), F32),
            jax.ShapeDtypeStruct((SC * Y, X), F32),
        ),
        in_specs=[hbm, hbm, hbm, hbm],
        out_specs=(vmem, vmem, vmem),
        scratch_shapes=[
            pltpu.VMEM((SC * Y, X), F32),
            pltpu.SMEM(beams.shape, F32),
            pltpu.SMEM(chan_bins.shape, jnp.int32),
            pltpu.VMEM((Y, X), jnp.int32),
            pltpu.VMEM((KP, LANES), F32),
            pltpu.VMEM((K3, 2 * DEPTHS), F32),
            pltpu.VMEM((2 * DEPTHS, K3), BF16),
            pltpu.VMEM((2 * KP, 2 * DEPTHS), BF16),
            pltpu.VMEM((KP, N), F32),
            pltpu.VMEM((2 * DEPTHS, N), BF16),
            pltpu.VMEM((2 * DEPTHS, N), BF16),
            pltpu.VMEM((KP, N), F32),
            pltpu.VMEM(((SC + 1) * (Y + 2 * HALF), LANES), F32),
            pltpu.VMEM(((SC + 1) * Y, LANES), F32),
            pltpu.VMEM(((SC + 1) * Y, LANES), F32),
        ]
        + [block] * 9
        + [dma((2, G)), dma((2, G)), dma((2, G, NCH)), dma((2, G, NCH)), dma((2, G, NCH)), dma((4,))],
        compiler_params=pltpu.CompilerParams(
            collective_id=0, has_side_effects=True, vmem_limit_bytes=40 * 1024 * 1024
        ),
    )(*(pltpu.with_memory_space_constraint(arg, pltpu.HBM) for arg in args))
    spectrum, residual = pl.pallas_call(
        functools.partial(finish_kernel, R),
        out_shape=(
            jax.ShapeDtypeStruct((2 * DEPTHS * R, LANES), F32),
            jax.ShapeDtypeStruct((SC * Y, X), F32),
        ),
        in_specs=[vmem, vmem, vmem],
        out_specs=(hbm, hbm),
        scratch_shapes=[pltpu.VMEM((2 * DEPTHS * R + 8, LANES), F32), dma((1 + 2 * PARTS,))],
        compiler_params=pltpu.CompilerParams(vmem_limit_bytes=8 * 1024 * 1024),
    )(update, first, cells)
    return spectrum.reshape(2, DEPTHS, 1, N), residual.reshape(dirty.shape)


def solution(mesh):
    placed = (P(None, "chan", "tile", None), P("chan", None), P(), P("tile", None))
    return jax.shard_map(
        on_device,
        mesh=mesh,
        in_specs=placed,
        out_specs=(P(None, None, "tile", "chan"), P(None, "chan", "tile", None)),
        check_vma=False,
    )
```

profile of v0, /device:TPU:0, one launch (start us, length us, event | category | flops | bytes accessed | tf_op | source)
XLA Modules:
  0.0 22.4 jit_solution(4225594173807583962)
XLA Ops:
  0.6 20.5 %shard_map.59 = (f32[512,512]{1,0:T(8,128)S(1)}, f32[512,512]{1,0:T(8,128)S(1)}, f32[288,128]{1,0:T(8,128)S(1)}) custom-call(f32[288,128]{1,0:T(8,128)} %bitcast.4, f32[9,289]{1,0:T(8,128)} %beams_hbm.1, s32[36]{0:T(128)} %bins_hbm.1, s32[16,128]{1,0:T(8,128)} %bitcast.5), custom_call_target="tpu_custom_call" | custom-call | tf_op jit(solution)/shard_map/pallas_call | solution.py:452
  21.1 1.2 %shard_map.60 = (f32[2048,128]{1,0:T(8,128)}, f32[288,128]{1,0:T(8,128)}) custom-call(f32[512,512]{1,0:T(8,128)S(1)} %get-tuple-element.7.update, f32[512,512]{1,0:T(8,128)S(1)} %get-tuple-element.8.first, f32[288,128]{1,0:T(8,128)S(1)} %get-tuple-element.9.cells), custom_call_target="tpu_custom_call" | custom-call | tf_op jit(solution)/shard_map/pallas_call | solution.py:484
where the time goes:
time: 22.5 us; the launch traced here: 22.4 us
  Pallas kernels  21.7 us (96%)
  between operations  0.64 us (3%)
    pallas_call x1, Pallas kernels, on_device(): pl.pallas_call(functools.partial(kernel, d), out_shape=(jax.ShapeDtypeStr...  20.5 us
    pallas_call x1, Pallas kernels, on_device(): pl.pallas_call(functools.partial(finish_kernel, R), out_shape=(jax.ShapeD...  1.23 us

commit v1 on v0

--- a/solution.py
+++ b/solution.py
@@ -14,6 +14,7 @@
 STEP_SIZE = 0.5
 MESH = pl.DeviceIdType.MESH
 LANES = 128
+REACH = 2
 F32 = jnp.float32
 BF16 = jnp.bfloat16
 
@@ -31,6 +32,11 @@
     squared = a * a + b * b
     factor = jnp.maximum(1.0 - THRESHOLD * lax.rsqrt(jnp.maximum(squared, 1e-30)), 0.0)
     return a * factor, b * factor
+
+
+def hops(half):
+    last = -((REACH - half) // (REACH + 1))
+    return [(REACH + 1) * m for m in range(-last, last + 1)]
 
 
 def aligned(row):
@@ -54,6 +60,9 @@
     beams,
     bins,
     order,
+    wide,
+    places,
+    bands,
     bincol,
     at3,
     a3,
@@ -178,6 +187,59 @@
     x[...] = jnp.zeros_like(x)
 
     shift = int(math.log2(LANES))
+    PY = Y + 2 * HALF
+    groups = hops(HALF)
+    GY = len(groups) * Y
+    near_lanes = list(range(-REACH, REACH + 1))
+    per = LANES // PY
+    wide[...] = jnp.zeros_like(wide)
+    CP = round_up(C, 8)
+    chunks = wide.shape[0] // CP
+    for m in range(chunks):
+        size = min(LANES, BEAM * BEAM - m * LANES)
+        wide[m * CP : m * CP + C, 0:size] = beams[:, m * LANES : m * LANES + size]
+    lane8 = lax.broadcasted_iota(jnp.int32, (8, LANES), 1)
+    line8 = lax.broadcasted_iota(jnp.int32, (8, LANES), 0)
+    for n, turn in enumerate(groups):
+        low = -REACH if turn <= 0 else 0
+        high = REACH if turn >= 0 else 0
+        for y in range(0, Y, 8):
+            i = lax.rem(lane8, PY) - (line8 + y)
+            for block in range(2):
+                j0 = lane8 // PY - REACH if block == 0 else jnp.where(lane8 < 2 * PY, REACH, LANES)
+                j = j0 + (HALF + turn)
+                ok = (i >= 0) & (i < BEAM) & (j0 >= low) & (j0 <= high) & (j >= 0) & (j < BEAM)
+                places[pl.ds((block * len(groups) + n) * Y + y, 8), :] = jnp.where(ok, i * BEAM + j, -1)
+
+    def band(c, carry):
+        rows = [
+            jnp.broadcast_to(wide[pl.ds(m * CP + c, 1), :], (8, LANES)) for m in range(chunks)
+        ]
+        for n, turn in enumerate(groups):
+            parts = []
+            for block in range(2):
+                if block == 1 and turn < 0:
+                    parts.append((jnp.zeros((Y, LANES), BF16),) * 2)
+                    continue
+                halves = []
+                for y in range(0, Y, 8):
+                    place = places[pl.ds((block * len(groups) + n) * Y + y, 8), :]
+                    col = place & (LANES - 1)
+                    row = lax.shift_right_arithmetic(place, shift)
+                    acc = jnp.zeros((8, LANES), F32)
+                    for m, source in enumerate(rows):
+                        taken = jnp.take_along_axis(source, col, axis=1, mode="promise_in_bounds")
+                        acc = jnp.where(row == m, taken, acc)
+                    halves.append(acc)
+                parts.append(split(jnp.concatenate(halves, axis=0)))
+            for h in range(2):
+                target = pl.ds(pl.multiple_of(c * (2 * GY) + h * GY + n * Y, 16), Y)
+                bands[target, 0:LANES] = parts[0][h]
+                bands[target, LANES : 2 * LANES] = parts[0][h]
+                bands[target, 2 * LANES : 3 * LANES] = parts[1][h]
+        return carry
+
+    lax.fori_loop(0, C, band, 0)
 
     def permute(cells):
         halves = []
@@ -274,33 +336,32 @@
         copy.start()
     recv_d[g] = send_d[g]
 
-    PY = Y + 2 * HALF
-    lane = lax.broadcasted_iota(jnp.int32, (Y, LANES), 1)
-    blocks = [range(0, (BEAM + 1) // 2), range((BEAM + 1) // 2, BEAM)]
-
-    def convolve(c, carry):
-        totals = [jnp.zeros((Y, LANES), F32) for _ in range(S)]
-        for block in blocks:
-            sums = [[None] * len(block) for _ in range(S)]
-            for i in range(BEAM):
-                rows = [padded[pl.ds((c * S + s) * PY + i, Y), :] for s in range(S)]
-                for n, j in enumerate(block):
-                    tap = beams[c, i * BEAM + j]
-                    for s in range(S):
-                        term = tap * rows[s]
-                        sums[s][n] = term if i == 0 else sums[s][n] + term
-            for n, j in enumerate(block):
-                inside = jnp.logical_and(lane + (j - HALF) >= 0, lane + (j - HALF) < LANES)
-                for s in range(S):
-                    moved = sums[s][n]
-                    if j != HALF:
-                        moved = pltpu.roll(moved, (HALF - j) % LANES, axis=1)
-                        moved = jnp.where(inside, moved, 0.0)
-                    totals[s] = totals[s] + moved
+    lane = lax.broadcasted_iota(jnp.int32, (PY, LANES), 1)
+
+    def moved(rows, by):
+        if by == 0:
+            return rows
+        at = lane[: rows.shape[0]] + by
+        return jnp.where((at >= 0) & (at < LANES), pltpu.roll(rows, (-by) % LANES, axis=1), 0.0)
+
+    def convolve(c):
+        images = [padded[pl.ds((c * S + s) * PY, PY), :] for s in range(S)]
+        high, low = [], []
+        for by in near_lanes:
+            pairs = [split(moved(image, by)) for image in images]
+            high.append(jnp.concatenate([pair[0] for pair in pairs], axis=1))
+            low.append(jnp.concatenate([pair[1] for pair in pairs], axis=1))
+        rest = jnp.zeros((LANES - 2 * PY, S * LANES), BF16)
+        right = jnp.concatenate(high[:per] + low[:per] + high[per:] + low[per:] + [rest], axis=0)
+        sums = mxu(bands[c * 2 * GY : (c + 1) * 2 * GY, :], right)
         for s in range(S):
-            cells = pl.ds(aligned((s * C + c) * Y), Y)
-            res[cells, :] = dirty[cells, :] - totals[s]
-        return carry
+            total = None
+            for n, turn in enumerate(groups):
+                span, lanes = slice(n * Y, (n + 1) * Y), slice(s * LANES, (s + 1) * LANES)
+                term = moved(sums[span, lanes] + sums[GY + n * Y : GY + (n + 1) * Y, lanes], turn)
+                total = term if total is None else total + term
+            cells = pl.ds((s * C + c) * Y, Y)
+            res[cells, :] = dirty[cells, :] - total
 
     def gather_res(c, carry):
         for s in range(S):
@@ -328,10 +389,6 @@
             recv_h[q, k] = jnp.zeros(recv_h.shape[2:], F32)
 
     copies_r = []
-
-    def step(c, carry):
-        gather_res(c - 1, 0)
-        return convolve(c, carry)
 
     def send_slots(k):
         pack(send_r, k, slots)
@@ -355,14 +412,11 @@
                 padded[pl.ds(k * W * PY + at_row + r, W, stride=PY), :] = recv_h[
                     q, k, r * W : r * W + W, :
                 ]
-        if k == 0:
-            convolve(0, 0)
-        else:
-            step(k * CC, 0)
-            send_slots(k - 1)
-        lax.fori_loop(k * CC + 1, (k + 1) * CC, step, 0)
-    gather_res(C - 1, 0)
-    send_slots(NCH - 1)
+        for c in range(k * CC, (k + 1) * CC):
+            convolve(c)
+        for c in range(k * CC, (k + 1) * CC):
+            gather_res(c, 0)
+        send_slots(k)
 
     for copy in in_d:
         copy.wait_recv()
@@ -460,9 +514,12 @@
         out_specs=(vmem, vmem, vmem),
         scratch_shapes=[
             pltpu.VMEM((SC * Y, X), F32),
-            pltpu.SMEM(beams.shape, F32),
+            pltpu.VMEM(beams.shape, F32),
             pltpu.SMEM(chan_bins.shape, jnp.int32),
             pltpu.VMEM((Y, X), jnp.int32),
+            pltpu.VMEM((pl.cdiv(beams.shape[1], LANES) * round_up(C, 8), LANES), F32),
+            pltpu.VMEM((2 * len(hops(HALF)) * Y, LANES), jnp.int32),
+            pltpu.VMEM((C * 2 * len(hops(HALF)) * Y, 3 * LANES), BF16),
             pltpu.VMEM((KP, LANES), F32),
             pltpu.VMEM((K3, 2 * DEPTHS), F32),
             pltpu.VMEM((2 * DEPTHS, K3), BF16),

time: 22.5 us -> 21 us (0.933)
  Pallas kernels: 21.7 us -> 20.3 us
    pallas_call x1, Pallas kernels: 20.5 us -> 19 us  [on_device(): pl.pallas_call(functools.partial(kernel, d), out_shape=(jax.ShapeDtypeStr...]
where the time goes in v1:
time: 21 us; the launch traced here: 20.9 us
  Pallas kernels  20.3 us (97%)
  between operations  0.64 us (3%)
    pallas_call x1, Pallas kernels, on_device(): pl.pallas_call(functools.partial(kernel, d), out_shape=(jax.ShapeDtypeStr...  19 us
    pallas_call x1, Pallas kernels, on_device(): pl.pallas_call(functools.partial(finish_kernel, R), out_shape=(jax.ShapeD...  1.23 us

profile of v1, /device:TPU:0, one launch (start us, length us, event | category | flops | bytes accessed | tf_op | source)
XLA Modules:
  0.0 20.9 jit_solution(404117327606339074)
XLA Ops:
  0.6 19.0 %shard_map.59 = (f32[512,512]{1,0:T(8,128)S(1)}, f32[512,512]{1,0:T(8,128)S(1)}, f32[288,128]{1,0:T(8,128)S(1)}) custom-call(f32[288,128]{1,0:T(8,128)} %bitcast.4, f32[9,289]{1,0:T(8,128)} %beams_hbm.1, s32[36]{0:T(128)} %bins_hbm.1, s32[16,128]{1,0:T(8,128)} %bitcast.5), custom_call_target="tpu_custom_call" | custom-call | tf_op jit(solution)/shard_map/pallas_call | solution.py:506
  19.7 1.2 %shard_map.60 = (f32[2048,128]{1,0:T(8,128)}, f32[288,128]{1,0:T(8,128)}) custom-call(f32[512,512]{1,0:T(8,128)S(1)} %get-tuple-element.7.update, f32[512,512]{1,0:T(8,128)S(1)} %get-tuple-element.8.first, f32[288,128]{1,0:T(8,128)S(1)} %get-tuple-element.9.cells), custom_call_target="tpu_custom_call" | custom-call | tf_op jit(solution)/shard_map/pallas_call | solution.py:541

commit v2 on v1

--- a/solution.py
+++ b/solution.py
@@ -83,12 +83,14 @@
     recv_m,
     recv_h,
     recv_r,
-    sems_a,
-    sems_d,
-    sems_m,
-    sems_h,
-    sems_r,
+    sent,
+    got_a,
+    got_d,
+    got_m,
+    got_h,
+    got_r,
     sems_in,
+    joined,
 ):
     G, T, R, Y, C, S, W, CC, NCH, HALF, BEAM = (
         d["G"], d["T"], d["R"], d["Y"], d["C"], d["S"], d["W"], d["CC"], d["NCH"], d["HALF"], d["BEAM"]
@@ -106,19 +108,13 @@
     loads = [pltpu.make_async_copy(src, dst, sems_in.at[n]) for n, (src, dst) in enumerate(pairs)]
     for load in loads:
         load.start()
+    last, lead = G - 1, G - 2
     barrier = pltpu.get_barrier_semaphore()
-    for step in range(1, G):
-        pl.semaphore_signal(barrier, inc=1, device_id=(lax.rem(g + step, G), t), device_id_type=MESH)
-
-    @pl.when(has_prev)
-    def _():
-        for p in range(G):
-            pl.semaphore_signal(barrier, inc=1, device_id=(p, before), device_id_type=MESH)
-
-    @pl.when(has_next)
-    def _():
-        for p in range(G):
-            pl.semaphore_signal(barrier, inc=1, device_id=(p, after), device_id_type=MESH)
+    for p in range(last):
+
+        @pl.when(g != p)
+        def _():
+            pl.semaphore_signal(barrier, inc=1, device_id=(p, t), device_id_type=MESH)
 
     def pack(send, k, cells):
         for p in range(G):
@@ -131,26 +127,41 @@
             mixed[(c * S + s) * Y : (c * S + s) * Y + Y, :] = dirty[(s * C + c) * Y : (s * C + c) * Y + Y, :]
     for k in range(NCH):
         pack(send_a, k, mixed)
-    near = has_prev.astype(jnp.int32) + has_next.astype(jnp.int32)
-    pl.semaphore_wait(barrier, G - 1 + G * near)
-
-    def own_copies(src, dst, sems, *k):
-        out_copies, in_copies = [], []
+    @pl.when(g != last)
+    def _():
+        pl.semaphore_wait(barrier, G - 1)
+
+    @pl.when(g == lead)
+    def _():
+        pl.semaphore_signal(joined, inc=1, device_id=(last, t), device_id_type=MESH)
+
+        @pl.when(has_prev)
+        def _():
+            pl.semaphore_signal(barrier, inc=1, device_id=(last, before), device_id_type=MESH)
+
+        @pl.when(has_next)
+        def _():
+            pl.semaphore_signal(barrier, inc=1, device_id=(last, after), device_id_type=MESH)
+
+    @pl.when(g == last)
+    def _():
+        pl.semaphore_wait(joined, 1)
+
+    def own_copies(src, dst, kind, got):
+        copies = []
         for step in range(1, G):
             p = lax.rem(g + step, G)
-            out_copies.append(
+            copies.append(
                 pltpu.make_async_remote_copy(
-                    src(p), dst(g), sems.at[(0, p, *k)], sems.at[(1, g, *k)], device_id=(p, t), device_id_type=MESH
+                    src(p), dst(g), sent.at[kind], got, device_id=(p, t), device_id_type=MESH
                 )
             )
-            in_copies.append(
-                pltpu.make_async_remote_copy(
-                    src(p), dst(p), sems.at[(0, p, *k)], sems.at[(1, p, *k)], device_id=(p, t), device_id_type=MESH
-                )
-            )
-        return out_copies, in_copies
-
-    out_a, in_a = own_copies(lambda p: send_a.at[p], lambda p: recv_a.at[p], sems_a)
+        return copies
+
+    def await_bytes(ref, sem):
+        pltpu.make_async_copy(ref, ref, sem).wait()
+
+    out_a = own_copies(lambda p: send_a.at[p], lambda p: recv_a.at[p], 0, got_a.at[0])
     for copy in out_a:
         copy.start()
     recv_a[g] = send_a[g]
@@ -276,8 +287,13 @@
 
     BLOCK = 16
 
-    for copy in in_a:
-        copy.wait_recv()
+    @pl.when(g == last)
+    def _():
+        pl.semaphore_wait(barrier, has_prev.astype(jnp.int32) + has_next.astype(jnp.int32))
+        for p in range(last):
+            pl.semaphore_signal(joined, inc=1, device_id=(p, t), device_id_type=MESH)
+
+    await_bytes(recv_a.at[0:last], got_a.at[0])
     project(recv_a)
 
     def shrink_first(i, carry):
@@ -295,7 +311,12 @@
     up = g * R < HALF
     goes = jnp.logical_or(jnp.logical_and(up, has_prev), jnp.logical_and(jnp.logical_not(up), has_next))
     toward = jnp.where(up, before, after)
-    copies_m, copies_h = [], []
+    copies_h = []
+
+    @pl.when(g != last)
+    def _():
+        pl.semaphore_wait(joined, 1)
+
     for k in range(NCH):
         for p in range(G):
             for r in range(R):
@@ -306,8 +327,8 @@
             pltpu.make_async_remote_copy(
                 send_m.at[p, k],
                 recv_h.at[g, k],
-                sems_h.at[0, p, k],
-                sems_h.at[1, g, k],
+                sent.at[4],
+                got_h.at[up.astype(jnp.int32), k],
                 device_id=(p, toward),
                 device_id_type=MESH,
             )
@@ -320,19 +341,14 @@
             for copy in halo:
                 copy.start()
 
-        copies = own_copies(
-            lambda p: send_m.at[p, k], lambda p: recv_m.at[p, k], sems_m, k
-        )
-        copies_m.append(copies)
-        for copy in copies[0]:
+        for copy in own_copies(lambda p: send_m.at[p, k], lambda p: recv_m.at[p, k], 2, got_m.at[k]):
             copy.start()
         recv_m[g, k] = send_m[g, k]
 
     lax.fori_loop(0, C, gather_dirty, 0)
     for k in range(NCH):
         pack(send_d, k, slots)
-    out_d, in_d = own_copies(lambda p: send_d.at[p], lambda p: recv_d.at[p], sems_d)
-    for copy in out_d:
+    for copy in own_copies(lambda p: send_d.at[p], lambda p: recv_d.at[p], 1, got_d.at[0]):
         copy.start()
     recv_d[g] = send_d[g]
 
@@ -370,40 +386,29 @@
             slots[target, :] = permute(lambda y: jnp.broadcast_to(res[pl.ds(source + y, 1), :], (8, LANES)))
         return carry
 
-    def halo_block(q, k, ok):
-        arrived = pltpu.make_async_remote_copy(
-            send_m.at[q, k],
-            recv_h.at[q, k],
-            sems_h.at[0, q, k],
-            sems_h.at[1, q, k],
-            device_id=(q, t),
-            device_id_type=MESH,
-        )
+    def halo_blocks(first, end, side, k, ok):
+        blocks = recv_h.at[first:end, k]
 
         @pl.when(ok)
         def _():
-            arrived.wait_recv()
+            await_bytes(blocks, got_h.at[side, k])
 
         @pl.when(jnp.logical_not(ok))
         def _():
-            recv_h[q, k] = jnp.zeros(recv_h.shape[2:], F32)
-
-    copies_r = []
+            blocks[...] = jnp.zeros(blocks.shape, F32)
 
     def send_slots(k):
         pack(send_r, k, slots)
-        copies = own_copies(lambda p: send_r.at[p, k], lambda p: recv_r.at[p, k], sems_r, k)
-        copies_r.append(copies)
-        for copy in copies[0]:
+        for copy in own_copies(lambda p: send_r.at[p, k], lambda p: recv_r.at[p, k], 3, got_r.at[k]):
             copy.start()
         recv_r[g, k] = send_r[g, k]
 
     for k in range(NCH):
-        for copy in copies_m[k][1]:
-            copy.wait_recv()
+        await_bytes(recv_m.at[0:last, k], got_m.at[k])
+        halo_blocks(0, HALF // R, 1, k, has_next)
+        halo_blocks(HALF // R, G, 0, k, has_prev)
         for q in range(G):
             from_next = q * R < HALF
-            halo_block(q, k, has_next if from_next else has_prev)
             at_row = Y + HALF + q * R if from_next else q * R - HALF
             for r in range(R):
                 padded[pl.ds(k * W * PY + HALF + q * R + r, W, stride=PY), :] = recv_m[
@@ -418,8 +423,7 @@
             gather_res(c, 0)
         send_slots(k)
 
-    for copy in in_d:
-        copy.wait_recv()
+    await_bytes(recv_d.at[0:last], got_d.at[0])
     project(recv_d)
 
     def shrink_slots(i, carry):
@@ -431,21 +435,15 @@
     lax.fori_loop(0, DEPTHS // BLOCK, shrink_slots, 0)
 
     for k in range(NCH):
-        for copy in copies_r[k][1]:
-            copy.wait_recv()
+        await_bytes(recv_r.at[0:last, k], got_r.at[k])
     project(recv_r)
 
-    for copy in out_a + out_d:
-        copy.wait_send()
-    for k in range(NCH):
-        for copy in copies_m[k][0] + copies_r[k][0]:
-            copy.wait_send()
+    for kind, ref in enumerate((send_a, send_d, send_m, send_r)):
+        await_bytes(ref.at[0:last], sent.at[kind])
 
     @pl.when(goes)
     def _():
-        for halo in copies_h:
-            for copy in halo:
-                copy.wait_send()
+        await_bytes(send_m, sent.at[4])
 
 
 PARTS = 4
@@ -533,7 +531,8 @@
             pltpu.VMEM(((SC + 1) * Y, LANES), F32),
         ]
         + [block] * 9
-        + [dma((2, G)), dma((2, G)), dma((2, G, NCH)), dma((2, G, NCH)), dma((2, G, NCH)), dma((4,))],
+        + [dma((5,)), dma((1,)), dma((1,)), dma((NCH,)), dma((2, NCH)), dma((NCH,)), dma((4,))]
+        + [pltpu.SemaphoreType.REGULAR],
         compiler_params=pltpu.CompilerParams(
             collective_id=0, has_side_effects=True, vmem_limit_bytes=40 * 1024 * 1024
         ),

time: 21 us -> 20 us (0.952)
  Pallas kernels: 20.3 us -> 19.2 us
    pallas_call x1, Pallas kernels: 19 us -> 17.9 us  [on_device(): pl.pallas_call(functools.partial(kernel, d), out_shape=(jax.ShapeDtypeStr...]
where the time goes in v2:
time: 20 us; the launch traced here: 19.8 us
  Pallas kernels  19.2 us (96%)
  between operations  0.64 us (3%)
    pallas_call x1, Pallas kernels, on_device(): pl.pallas_call(functools.partial(kernel, d), out_shape=(jax.ShapeDtypeStr...  17.9 us
    pallas_call x1, Pallas kernels, on_device(): pl.pallas_call(functools.partial(finish_kernel, R), out_shape=(jax.ShapeD...  1.23 us

profile of v2, /device:TPU:0, one launch (start us, length us, event | category | flops | bytes accessed | tf_op | source)
XLA Modules:
  0.0 19.8 jit_solution(7724445728604979277)
XLA Ops:
  0.6 17.9 %shard_map.59 = (f32[512,512]{1,0:T(8,128)S(1)}, f32[512,512]{1,0:T(8,128)S(1)}, f32[288,128]{1,0:T(8,128)S(1)}) custom-call(f32[288,128]{1,0:T(8,128)} %bitcast.4, f32[9,289]{1,0:T(8,128)} %beams_hbm.1, s32[36]{0:T(128)} %bins_hbm.1, s32[16,128]{1,0:T(8,128)} %bitcast.5), custom_call_target="tpu_custom_call" | custom-call | tf_op jit(solution)/shard_map/pallas_call | solution.py:504
  18.6 1.2 %shard_map.60 = (f32[2048,128]{1,0:T(8,128)}, f32[288,128]{1,0:T(8,128)}) custom-call(f32[512,512]{1,0:T(8,128)S(1)} %get-tuple-element.7.update, f32[512,512]{1,0:T(8,128)S(1)} %get-tuple-element.8.first, f32[288,128]{1,0:T(8,128)S(1)} %get-tuple-element.9.cells), custom_call_target="tpu_custom_call" | custom-call | tf_op jit(solution)/shard_map/pallas_call | solution.py:540

commit v3 on v2

--- a/solution.py
+++ b/solution.py
@@ -50,6 +50,7 @@
 def kernel(
     d,
     dirty_hbm,
+    blocks_hbm,
     beams_hbm,
     bins_hbm,
     order_hbm,
@@ -67,21 +68,14 @@
     at3,
     a3,
     at2,
-    x,
     first_hi,
     first_lo,
-    model,
     padded,
-    slots,
-    mixed,
-    send_a,
-    send_d,
+    slots_d,
+    slots_r,
     send_m,
-    send_r,
     recv_a,
     recv_d,
-    recv_m,
-    recv_h,
     recv_r,
     sent,
     got_a,
@@ -90,13 +84,16 @@
     got_h,
     got_r,
     sems_in,
+    sems_own,
     joined,
 ):
-    G, T, R, Y, C, S, W, CC, NCH, HALF, BEAM = (
-        d["G"], d["T"], d["R"], d["Y"], d["C"], d["S"], d["W"], d["CC"], d["NCH"], d["HALF"], d["BEAM"]
+    G, T, R, Y, C, S, CC, NCH, HALF, BEAM = (
+        d["G"], d["T"], d["R"], d["Y"], d["C"], d["S"], d["CC"], d["NCH"], d["HALF"], d["BEAM"]
     )
     SC = S * C
     KP = d["KP"]
+    X = LANES
+    PY = Y + 2 * HALF
     g = lax.axis_index("chan")
     t = lax.axis_index("tile")
     has_prev = t > 0
@@ -106,8 +103,14 @@
 
     pairs = ((dirty_hbm, dirty), (bins_hbm, bins), (beams_hbm, beams), (order_hbm, order))
     loads = [pltpu.make_async_copy(src, dst, sems_in.at[n]) for n, (src, dst) in enumerate(pairs)]
+    from_a, from_d, from_r = (ref.reshape(G, S, C, R, X) for ref in (recv_a, recv_d, recv_r))
+    to_d, to_r = (ref.reshape(S, C, G, R, X) for ref in (slots_d, slots_r))
+    to_m = send_m.reshape(G, S, C, R, X)
+    rows = padded.reshape(S, C, PY // R, R, X)
+    own_a = pltpu.make_async_copy(blocks_hbm.at[:, :, g], from_a.at[g], sems_own.at[0])
     for load in loads:
         load.start()
+    own_a.start()
     last, lead = G - 1, G - 2
     barrier = pltpu.get_barrier_semaphore()
     for p in range(last):
@@ -116,17 +119,13 @@
         def _():
             pl.semaphore_signal(barrier, inc=1, device_id=(p, t), device_id_type=MESH)
 
-    def pack(send, k, cells):
-        for p in range(G):
-            for r in range(R):
-                send[p, k, r * W : r * W + W, :] = cells[pl.ds(k * W * Y + p * R + r, W, stride=Y), :]
-
-    loads[0].wait()
-    for c in range(C):
-        for s in range(S):
-            mixed[(c * S + s) * Y : (c * S + s) * Y + Y, :] = dirty[(s * C + c) * Y : (s * C + c) * Y + Y, :]
-    for k in range(NCH):
-        pack(send_a, k, mixed)
+    for edge, start in ((has_prev, 0), (has_next, Y + HALF)):
+
+        @pl.when(jnp.logical_not(edge))
+        def _():
+            for image in range(SC):
+                padded[image * PY + start : image * PY + start + HALF, :] = jnp.zeros((HALF, X), F32)
+
     @pl.when(g != last)
     def _():
         pl.semaphore_wait(barrier, G - 1)
@@ -161,16 +160,45 @@
     def await_bytes(ref, sem):
         pltpu.make_async_copy(ref, ref, sem).wait()
 
-    out_a = own_copies(lambda p: send_a.at[p], lambda p: recv_a.at[p], 0, got_a.at[0])
-    for copy in out_a:
+    for copy in own_copies(lambda p: blocks_hbm.at[:, :, p], lambda p: from_a.at[p], 0, got_a.at[0]):
         copy.start()
-    recv_a[g] = send_a[g]
-
-    for load in loads[1:]:
+
+    for load in loads:
         load.wait()
+    shift = int(math.log2(LANES))
+
+    def permute(cells):
+        halves = []
+        for h in range(Y // 8):
+            pixel = order[8 * h : 8 * h + 8, :]
+            col = pixel & (LANES - 1)
+            row = lax.shift_right_logical(pixel, shift)
+            acc = jnp.zeros((8, LANES), F32)
+            for y in range(Y):
+                taken = jnp.take_along_axis(cells(y), col, axis=1, mode="promise_in_bounds")
+                acc = jnp.where(row == y, taken, acc)
+            halves.append(acc)
+        return jnp.concatenate(halves, axis=0)
+
+    def gather_dirty(c, carry):
+        for s in range(S):
+            source = (s * C + c) * Y
+            slots_d[pl.ds(aligned(source), Y), :] = permute(
+                lambda y: jnp.broadcast_to(dirty[pl.ds(source + y, 1), :], (8, LANES))
+            )
+        return carry
+
+    lax.fori_loop(0, C, gather_dirty, 0)
+    for copy in own_copies(lambda p: to_d.at[:, :, p], lambda p: from_d.at[p], 1, got_d.at[0]):
+        copy.start()
+    own_d = pltpu.make_async_copy(to_d.at[:, :, g], from_d.at[g], sems_own.at[1])
+    own_d.start()
     bincol[...] = jnp.zeros_like(bincol)
-    for row in range(G * C):
-        bincol[S * row : S * row + S, :] = jnp.full((S, LANES), bins[row].astype(F32))
+    for q in range(G):
+        for c in range(C):
+            for s in range(S):
+                row = q * SC + s * C + c
+                bincol[row : row + 1, :] = jnp.full((1, LANES), bins[q * C + c].astype(F32))
     scale = 1.0 / math.sqrt(G * C)
     at3[...] = jnp.zeros_like(at3)
     for piece in range(DEPTHS // LANES):
@@ -182,7 +210,7 @@
         turns = jnp.where(turns >= BINS, turns - BINS, turns)
         angles = turns * (2.0 * math.pi / BINS)
         row = lax.broadcasted_iota(jnp.int32, shape, 0)
-        is_q = (row & 1) == 0
+        is_q = lax.rem(row, SC) < C
         real = row < G * SC
         cosine = jnp.where(real, jnp.cos(angles) * scale, 0.0)
         sine = jnp.where(real, jnp.sin(angles) * scale, 0.0)
@@ -194,11 +222,12 @@
             at3[0:KP, lanes] = high.astype(F32)
             at3[KP : 2 * KP, lanes] = low.astype(F32)
             at3[2 * KP : 3 * KP, lanes] = high.astype(F32)
-    a3[...] = at3[...].T.astype(BF16)
-    x[...] = jnp.zeros_like(x)
-
-    shift = int(math.log2(LANES))
-    PY = Y + 2 * HALF
+    turned = at3[...].T.astype(BF16)
+    for n in range(DEPTHS // 16):
+        for half in range(2):
+            span = pl.ds((2 * n + half) * 16, 16)
+            a3[span, :] = turned[half * DEPTHS + n * 16 : half * DEPTHS + n * 16 + 16, :]
+
     groups = hops(HALF)
     GY = len(groups) * Y
     near_lanes = list(range(-REACH, REACH + 1))
@@ -250,40 +279,22 @@
                 bands[target, 2 * LANES : 3 * LANES] = parts[1][h]
         return carry
 
-    lax.fori_loop(0, C, band, 0)
-
-    def permute(cells):
-        halves = []
-        for h in range(Y // 8):
-            pixel = order[8 * h : 8 * h + 8, :]
-            col = pixel & (LANES - 1)
-            row = lax.shift_right_logical(pixel, shift)
-            acc = jnp.zeros((8, LANES), F32)
-            for y in range(Y):
-                taken = jnp.take_along_axis(cells(y), col, axis=1, mode="promise_in_bounds")
-                acc = jnp.where(row == y, taken, acc)
-            halves.append(acc)
-        return jnp.concatenate(halves, axis=0)
-
-    def gather_dirty(c, carry):
-        for s in range(S):
-            source = (s * C + c) * Y
-            target = pl.ds(aligned((c * S + s) * Y), Y)
-            slots[target, :] = permute(lambda y: jnp.broadcast_to(dirty[pl.ds(source + y, 1), :], (8, LANES)))
-        return carry
 
     def project(recv):
-        for q in range(G):
-            for k in range(NCH):
-                for r in range(R):
-                    x[q * SC + k * W : q * SC + k * W + W, r * LANES : (r + 1) * LANES] = recv[
-                        q, k, r * W : r * W + W, :
-                    ]
-        high, low = split(x[...])
+        blank = jnp.zeros((KP - G * SC, LANES), F32)
+        columns = [recv[pl.ds(r, G * SC, stride=R), :] for r in range(R)]
+        if KP > G * SC:
+            columns = [jnp.concatenate([column, blank], axis=0) for column in columns]
+        high, low = split(jnp.concatenate(columns, axis=1))
         parts = [high, high, low]
         if d["K3"] > 3 * KP:
-            parts.append(jnp.zeros((d["K3"] - 3 * KP, x.shape[1]), BF16))
-        big[...] = mxu(a3[...], jnp.concatenate(parts, axis=0))
+            parts.append(jnp.zeros((d["K3"] - 3 * KP, R * LANES), BF16))
+        return mxu(a3[...], jnp.concatenate(parts, axis=0))
+
+    def pairs_of(product):
+        for n in range(DEPTHS // BLOCK):
+            at = 2 * n * BLOCK
+            yield n * BLOCK, product[at : at + BLOCK, :], product[at + BLOCK : at + 2 * BLOCK, :]
 
     BLOCK = 16
 
@@ -293,40 +304,34 @@
         for p in range(last):
             pl.semaphore_signal(joined, inc=1, device_id=(p, t), device_id_type=MESH)
 
-    await_bytes(recv_a.at[0:last], got_a.at[0])
-    project(recv_a)
-
-    def shrink_first(i, carry):
-        top = pl.ds(pl.multiple_of(i * BLOCK, BLOCK), BLOCK)
-        low = pl.ds(pl.multiple_of(DEPTHS + i * BLOCK, BLOCK), BLOCK)
-        a, b = shrink_pair(big[top, :], big[low, :])
-        first_hi[top, :], first_lo[top, :] = split(a)
+    await_bytes(from_a.at[0:last], got_a.at[0])
+    own_a.wait()
+    for k, a, b in pairs_of(project(recv_a)):
+        a, b = shrink_pair(a, b)
+        first_hi[k : k + BLOCK, :], first_lo[k : k + BLOCK, :] = split(a)
+        low = slice(DEPTHS + k, DEPTHS + k + BLOCK)
         first_hi[low, :], first_lo[low, :] = split(b)
-        return carry
-
-    lax.fori_loop(0, DEPTHS // BLOCK, shrink_first, 0)
     both = mxu(at2[...], first_hi[...])
-    model[...] = both[:KP] + both[KP:] + mxu(at2[0:KP, :], first_lo[...])
+    model = both[:KP] + both[KP:] + mxu(at2[0:KP, :], first_lo[...])
+    for r in range(R):
+        send_m[pl.ds(r, G * SC, stride=R), :] = model[: G * SC, r * LANES : (r + 1) * LANES]
 
     up = g * R < HALF
     goes = jnp.logical_or(jnp.logical_and(up, has_prev), jnp.logical_and(jnp.logical_not(up), has_next))
     toward = jnp.where(up, before, after)
-    copies_h = []
+    copies_h, own_m, own_r = [], [], []
+    spot = jnp.where(up, (HALF + Y) // R + g, g - HALF // R)
+    chunks_of = [slice(k * CC, (k + 1) * CC) for k in range(NCH)]
 
     @pl.when(g != last)
     def _():
         pl.semaphore_wait(joined, 1)
 
     for k in range(NCH):
-        for p in range(G):
-            for r in range(R):
-                send_m[p, k, r * W : r * W + W, :] = model[
-                    p * SC + k * W : p * SC + k * W + W, r * LANES : (r + 1) * LANES
-                ]
         halo = [
             pltpu.make_async_remote_copy(
-                send_m.at[p, k],
-                recv_h.at[g, k],
+                to_m.at[p, :, chunks_of[k]],
+                rows.at[:, chunks_of[k], spot],
                 sent.at[4],
                 got_h.at[up.astype(jnp.int32), k],
                 device_id=(p, toward),
@@ -341,16 +346,21 @@
             for copy in halo:
                 copy.start()
 
-        for copy in own_copies(lambda p: send_m.at[p, k], lambda p: recv_m.at[p, k], 2, got_m.at[k]):
+        for copy in own_copies(
+            lambda p: to_m.at[p, :, chunks_of[k]],
+            lambda p: rows.at[:, chunks_of[k], HALF // R + p],
+            2,
+            got_m.at[k],
+        ):
             copy.start()
-        recv_m[g, k] = send_m[g, k]
-
-    lax.fori_loop(0, C, gather_dirty, 0)
-    for k in range(NCH):
-        pack(send_d, k, slots)
-    for copy in own_copies(lambda p: send_d.at[p], lambda p: recv_d.at[p], 1, got_d.at[0]):
-        copy.start()
-    recv_d[g] = send_d[g]
+        own_m.append(
+            pltpu.make_async_copy(
+                to_m.at[g, :, chunks_of[k]], rows.at[:, chunks_of[k], HALF // R + g], sems_own.at[2 + k]
+            )
+        )
+        own_m[k].start()
+
+    lax.fori_loop(0, C, band, 0)
 
     lane = lax.broadcasted_iota(jnp.int32, (PY, LANES), 1)
 
@@ -361,7 +371,7 @@
         return jnp.where((at >= 0) & (at < LANES), pltpu.roll(rows, (-by) % LANES, axis=1), 0.0)
 
     def convolve(c):
-        images = [padded[pl.ds((c * S + s) * PY, PY), :] for s in range(S)]
+        images = [padded[pl.ds((s * C + c) * PY, PY), :] for s in range(S)]
         high, low = [], []
         for by in near_lanes:
             pairs = [split(moved(image, by)) for image in images]
@@ -379,71 +389,58 @@
             cells = pl.ds((s * C + c) * Y, Y)
             res[cells, :] = dirty[cells, :] - total
 
-    def gather_res(c, carry):
+    def gather_res(c):
         for s in range(S):
             source = (s * C + c) * Y
-            target = pl.ds(aligned((c * S + s) * Y), Y)
-            slots[target, :] = permute(lambda y: jnp.broadcast_to(res[pl.ds(source + y, 1), :], (8, LANES)))
-        return carry
-
-    def halo_blocks(first, end, side, k, ok):
-        blocks = recv_h.at[first:end, k]
-
+            slots_r[pl.ds(source, Y), :] = permute(
+                lambda y: jnp.broadcast_to(res[pl.ds(source + y, 1), :], (8, LANES))
+            )
+
+    def await_halo(side, k, ok):
         @pl.when(ok)
         def _():
-            await_bytes(blocks, got_h.at[side, k])
-
-        @pl.when(jnp.logical_not(ok))
-        def _():
-            blocks[...] = jnp.zeros(blocks.shape, F32)
+            await_bytes(to_m.at[0 : HALF // R, :, chunks_of[k]], got_h.at[side, k])
 
     def send_slots(k):
-        pack(send_r, k, slots)
-        for copy in own_copies(lambda p: send_r.at[p, k], lambda p: recv_r.at[p, k], 3, got_r.at[k]):
+        for copy in own_copies(
+            lambda p: to_r.at[:, chunks_of[k], p], lambda p: from_r.at[p, :, chunks_of[k]], 3, got_r.at[k]
+        ):
             copy.start()
-        recv_r[g, k] = send_r[g, k]
+        own_r.append(
+            pltpu.make_async_copy(
+                to_r.at[:, chunks_of[k], g], from_r.at[g, :, chunks_of[k]], sems_own.at[2 + NCH + k]
+            )
+        )
+        own_r[k].start()
 
     for k in range(NCH):
-        await_bytes(recv_m.at[0:last, k], got_m.at[k])
-        halo_blocks(0, HALF // R, 1, k, has_next)
-        halo_blocks(HALF // R, G, 0, k, has_prev)
-        for q in range(G):
-            from_next = q * R < HALF
-            at_row = Y + HALF + q * R if from_next else q * R - HALF
-            for r in range(R):
-                padded[pl.ds(k * W * PY + HALF + q * R + r, W, stride=PY), :] = recv_m[
-                    q, k, r * W : r * W + W, :
-                ]
-                padded[pl.ds(k * W * PY + at_row + r, W, stride=PY), :] = recv_h[
-                    q, k, r * W : r * W + W, :
-                ]
+        await_bytes(to_m.at[0:last, :, chunks_of[k]], got_m.at[k])
+        own_m[k].wait()
+        await_halo(1, k, has_next)
+        await_halo(0, k, has_prev)
         for c in range(k * CC, (k + 1) * CC):
             convolve(c)
         for c in range(k * CC, (k + 1) * CC):
-            gather_res(c, 0)
+            gather_res(c)
         send_slots(k)
 
-    await_bytes(recv_d.at[0:last], got_d.at[0])
-    project(recv_d)
-
-    def shrink_slots(i, carry):
-        top = pl.ds(pl.multiple_of(i * BLOCK, BLOCK), BLOCK)
-        low = pl.ds(pl.multiple_of(DEPTHS + i * BLOCK, BLOCK), BLOCK)
-        first_slots[top, :], first_slots[low, :] = shrink_pair(big[top, :], big[low, :])
-        return carry
-
-    lax.fori_loop(0, DEPTHS // BLOCK, shrink_slots, 0)
+    await_bytes(from_d.at[0:last], got_d.at[0])
+    own_d.wait()
+    for k, a, b in pairs_of(project(recv_d)):
+        first_slots[k : k + BLOCK, :], first_slots[DEPTHS + k : DEPTHS + k + BLOCK, :] = shrink_pair(a, b)
 
     for k in range(NCH):
-        await_bytes(recv_r.at[0:last, k], got_r.at[k])
-    project(recv_r)
-
-    for kind, ref in enumerate((send_a, send_d, send_m, send_r)):
-        await_bytes(ref.at[0:last], sent.at[kind])
+        await_bytes(from_r.at[0:last, :, chunks_of[k]], got_r.at[k])
+        own_r[k].wait()
+    for k, a, b in pairs_of(project(recv_r)):
+        big[k : k + BLOCK, :], big[DEPTHS + k : DEPTHS + k + BLOCK, :] = a, b
+
+    for kind in range(4):
+        await_bytes(from_a.at[0:last], sent.at[kind])
 
     @pl.when(goes)
     def _():
-        await_bytes(send_m, sent.at[4])
+        await_bytes(from_a, sent.at[4])
 
 
 PARTS = 4
@@ -489,18 +486,17 @@
     R = Y // G
     CC = 3 if C % 3 == 0 else C
     NCH = C // CC
-    W = S * CC
     SC = S * C
     KP = round_up(G * SC, 16)
     K3 = round_up(3 * KP, LANES)
-    PB = round_up(R * W, 8)
     N = R * X
-    d = dict(G=G, T=T, R=R, Y=Y, C=C, S=S, W=W, CC=CC, NCH=NCH, HALF=HALF, BEAM=BEAM, KP=KP, K3=K3)
+    d = dict(G=G, T=T, R=R, Y=Y, C=C, S=S, CC=CC, NCH=NCH, HALF=HALF, BEAM=BEAM, KP=KP, K3=K3)
     vmem = pl.BlockSpec(memory_space=pltpu.VMEM)
     hbm = pl.BlockSpec(memory_space=pltpu.HBM)
-    block = pltpu.VMEM((G, NCH, PB, LANES), F32)
+    share = pltpu.VMEM((G * SC * R, LANES), F32)
+    strip = pltpu.VMEM((SC * Y, LANES), F32)
     dma = pltpu.SemaphoreType.DMA
-    args = (dirty.reshape(SC * Y, X), beams, chan_bins, pixel_order.reshape(Y, X))
+    args = (dirty.reshape(SC * Y, X), dirty.reshape(S, C, G, R, X), beams, chan_bins, pixel_order.reshape(Y, X))
     update, first, cells = pl.pallas_call(
         functools.partial(kernel, d),
         out_shape=(
@@ -508,7 +504,7 @@
             jax.ShapeDtypeStruct((2 * DEPTHS, N), F32),
             jax.ShapeDtypeStruct((SC * Y, X), F32),
         ),
-        in_specs=[hbm, hbm, hbm, hbm],
+        in_specs=[hbm, hbm, hbm, hbm, hbm],
         out_specs=(vmem, vmem, vmem),
         scratch_shapes=[
             pltpu.VMEM((SC * Y, X), F32),
@@ -522,16 +518,14 @@
             pltpu.VMEM((K3, 2 * DEPTHS), F32),
             pltpu.VMEM((2 * DEPTHS, K3), BF16),
             pltpu.VMEM((2 * KP, 2 * DEPTHS), BF16),
-            pltpu.VMEM((KP, N), F32),
             pltpu.VMEM((2 * DEPTHS, N), BF16),
             pltpu.VMEM((2 * DEPTHS, N), BF16),
-            pltpu.VMEM((KP, N), F32),
-            pltpu.VMEM(((SC + 1) * (Y + 2 * HALF), LANES), F32),
-            pltpu.VMEM(((SC + 1) * Y, LANES), F32),
-            pltpu.VMEM(((SC + 1) * Y, LANES), F32),
+            pltpu.VMEM((SC * (Y + 2 * HALF), LANES), F32),
+            strip,
+            strip,
         ]
-        + [block] * 9
-        + [dma((5,)), dma((1,)), dma((1,)), dma((NCH,)), dma((2, NCH)), dma((NCH,)), dma((4,))]
+        + [share] * 4
+        + [dma((5,)), dma((1,)), dma((1,)), dma((NCH,)), dma((2, NCH)), dma((NCH,)), dma((4,)), dma((2 + 2 * NCH,))]
         + [pltpu.SemaphoreType.REGULAR],
         compiler_params=pltpu.CompilerParams(
             collective_id=0, has_side_effects=True, vmem_limit_bytes=40 * 1024 * 1024

time: 20 us -> 19.4 us (0.970)
  Pallas kernels: 19.2 us -> 18.6 us
    pallas_call x1, Pallas kernels: 17.9 us -> 17.4 us  [on_device(): pl.pallas_call(functools.partial(kernel, d), out_shape=(jax.ShapeDtypeStr...]
where the time goes in v3:
time: 19.4 us; the launch traced here: 19.3 us
  Pallas kernels  18.6 us (96%)
  between operations  0.64 us (3%)
    pallas_call x1, Pallas kernels, on_device(): pl.pallas_call(functools.partial(kernel, d), out_shape=(jax.ShapeDtypeStr...  17.4 us
    pallas_call x1, Pallas kernels, on_device(): pl.pallas_call(functools.partial(finish_kernel, R), out_shape=(jax.ShapeD...  1.23 us

profile of v3, /device:TPU:0, one launch (start us, length us, event | category | flops | bytes accessed | tf_op | source)
XLA Modules:
  0.0 19.3 jit_solution(11669774763124807583)
XLA Ops:
  0.6 17.4 %shard_map.59 = (f32[512,512]{1,0:T(8,128)S(1)}, f32[512,512]{1,0:T(8,128)S(1)}, f32[288,128]{1,0:T(8,128)S(1)}) custom-call(f32[288,128]{1,0:T(8,128)} %bitcast.5, f32[2,9,4,4,128]{4,3,2,1,0:T(4,128)} %bitcast.6, f32[9,289]{1,0:T(8,128)} %beams_hbm.1, s32[36]{0:T(128)} %bins_hbm.1, s32[16,128]{1,0:T(8,128)} %bitcast.7), custom_call_target="tpu_custom_call" | custom-call | tf_op jit(solution)/shard_map/pallas_call | solution.py:500
  18.0 1.2 %shard_map.60 = (f32[2048,128]{1,0:T(8,128)}, f32[288,128]{1,0:T(8,128)}) custom-call(f32[512,512]{1,0:T(8,128)S(1)} %get-tuple-element.7.update, f32[512,512]{1,0:T(8,128)S(1)} %get-tuple-element.8.first, f32[288,128]{1,0:T(8,128)S(1)} %get-tuple-element.9.cells), custom_call_target="tpu_custom_call" | custom-call | tf_op jit(solution)/shard_map/pallas_call | solution.py:534

commit v4 on v3

--- a/solution.py
+++ b/solution.py
@@ -15,6 +15,7 @@
 MESH = pl.DeviceIdType.MESH
 LANES = 128
 REACH = 2
+BLOCK = 16
 F32 = jnp.float32
 BF16 = jnp.bfloat16
 
@@ -41,6 +42,12 @@
 
 def aligned(row):
     return row if isinstance(row, int) else pl.multiple_of(row, 8)
+
+
+def pairs_of(product):
+    for n in range(DEPTHS // BLOCK):
+        at = 2 * n * BLOCK
+        yield n * BLOCK, product[at : at + BLOCK, :], product[at + BLOCK : at + 2 * BLOCK, :]
 
 
 def mxu(a, b):
@@ -54,7 +61,8 @@
     beams_hbm,
     bins_hbm,
     order_hbm,
-    big,
+    right,
+    a3,
     first_slots,
     res,
     dirty,
@@ -66,7 +74,6 @@
     bands,
     bincol,
     at3,
-    a3,
     at2,
     first_hi,
     first_lo,
@@ -280,7 +287,7 @@
         return carry
 
 
-    def project(recv):
+    def stacked(recv):
         blank = jnp.zeros((KP - G * SC, LANES), F32)
         columns = [recv[pl.ds(r, G * SC, stride=R), :] for r in range(R)]
         if KP > G * SC:
@@ -289,14 +296,10 @@
         parts = [high, high, low]
         if d["K3"] > 3 * KP:
             parts.append(jnp.zeros((d["K3"] - 3 * KP, R * LANES), BF16))
-        return mxu(a3[...], jnp.concatenate(parts, axis=0))
-
-    def pairs_of(product):
-        for n in range(DEPTHS // BLOCK):
-            at = 2 * n * BLOCK
-            yield n * BLOCK, product[at : at + BLOCK, :], product[at + BLOCK : at + 2 * BLOCK, :]
-
-    BLOCK = 16
+        return jnp.concatenate(parts, axis=0)
+
+    def project(recv):
+        return mxu(a3[...], stacked(recv))
 
     @pl.when(g == last)
     def _():
@@ -319,7 +322,7 @@
     up = g * R < HALF
     goes = jnp.logical_or(jnp.logical_and(up, has_prev), jnp.logical_and(jnp.logical_not(up), has_next))
     toward = jnp.where(up, before, after)
-    copies_h, own_m, own_r = [], [], []
+    copies_h = []
     spot = jnp.where(up, (HALF + Y) // R + g, g - HALF // R)
     chunks_of = [slice(k * CC, (k + 1) * CC) for k in range(NCH)]
 
@@ -353,12 +356,9 @@
             got_m.at[k],
         ):
             copy.start()
-        own_m.append(
-            pltpu.make_async_copy(
-                to_m.at[g, :, chunks_of[k]], rows.at[:, chunks_of[k], HALF // R + g], sems_own.at[2 + k]
-            )
-        )
-        own_m[k].start()
+        pltpu.make_async_copy(
+            to_m.at[g, :, chunks_of[k]], rows.at[:, chunks_of[k], HALF // R + g], sems_own.at[2 + k]
+        ).start()
 
     lax.fori_loop(0, C, band, 0)
 
@@ -371,7 +371,7 @@
         return jnp.where((at >= 0) & (at < LANES), pltpu.roll(rows, (-by) % LANES, axis=1), 0.0)
 
     def convolve(c):
-        images = [padded[pl.ds((s * C + c) * PY, PY), :] for s in range(S)]
+        images = [padded[pl.ds(aligned((s * C + c) * PY), PY), :] for s in range(S)]
         high, low = [], []
         for by in near_lanes:
             pairs = [split(moved(image, by)) for image in images]
@@ -379,50 +379,48 @@
             low.append(jnp.concatenate([pair[1] for pair in pairs], axis=1))
         rest = jnp.zeros((LANES - 2 * PY, S * LANES), BF16)
         right = jnp.concatenate(high[:per] + low[:per] + high[per:] + low[per:] + [rest], axis=0)
-        sums = mxu(bands[c * 2 * GY : (c + 1) * 2 * GY, :], right)
+        sums = mxu(bands[pl.ds(pl.multiple_of(c * (2 * GY), 16), 2 * GY), :], right)
         for s in range(S):
             total = None
             for n, turn in enumerate(groups):
                 span, lanes = slice(n * Y, (n + 1) * Y), slice(s * LANES, (s + 1) * LANES)
                 term = moved(sums[span, lanes] + sums[GY + n * Y : GY + (n + 1) * Y, lanes], turn)
                 total = term if total is None else total + term
-            cells = pl.ds((s * C + c) * Y, Y)
+            cells = pl.ds(aligned((s * C + c) * Y), Y)
             res[cells, :] = dirty[cells, :] - total
 
     def gather_res(c):
         for s in range(S):
             source = (s * C + c) * Y
-            slots_r[pl.ds(source, Y), :] = permute(
+            slots_r[pl.ds(aligned(source), Y), :] = permute(
                 lambda y: jnp.broadcast_to(res[pl.ds(source + y, 1), :], (8, LANES))
             )
 
     def await_halo(side, k, ok):
         @pl.when(ok)
         def _():
-            await_bytes(to_m.at[0 : HALF // R, :, chunks_of[k]], got_h.at[side, k])
-
-    def send_slots(k):
+            await_bytes(to_m.at[0 : HALF // R, :, 0:CC], got_h.at[side, k])
+
+    def chunk(k, carry):
+        channels = pl.ds(k * CC, CC)
+        await_bytes(to_m.at[0:last, :, 0:CC], got_m.at[k])
+        await_bytes(to_m.at[0, :, 0:CC], sems_own.at[2 + k])
+        await_halo(1, k, has_next)
+        await_halo(0, k, has_prev)
+        for c in range(CC):
+            convolve(k * CC + c)
+        for c in range(CC):
+            gather_res(k * CC + c)
         for copy in own_copies(
-            lambda p: to_r.at[:, chunks_of[k], p], lambda p: from_r.at[p, :, chunks_of[k]], 3, got_r.at[k]
+            lambda p: to_r.at[:, channels, p], lambda p: from_r.at[p, :, channels], 3, got_r.at[k]
         ):
             copy.start()
-        own_r.append(
-            pltpu.make_async_copy(
-                to_r.at[:, chunks_of[k], g], from_r.at[g, :, chunks_of[k]], sems_own.at[2 + NCH + k]
-            )
-        )
-        own_r[k].start()
-
-    for k in range(NCH):
-        await_bytes(to_m.at[0:last, :, chunks_of[k]], got_m.at[k])
-        own_m[k].wait()
-        await_halo(1, k, has_next)
-        await_halo(0, k, has_prev)
-        for c in range(k * CC, (k + 1) * CC):
-            convolve(c)
-        for c in range(k * CC, (k + 1) * CC):
-            gather_res(c)
-        send_slots(k)
+        pltpu.make_async_copy(
+            to_r.at[:, channels, g], from_r.at[g, :, channels], sems_own.at[2 + NCH + k]
+        ).start()
+        return carry
+
+    lax.fori_loop(0, NCH, chunk, 0)
 
     await_bytes(from_d.at[0:last], got_d.at[0])
     own_d.wait()
@@ -431,9 +429,8 @@
 
     for k in range(NCH):
         await_bytes(from_r.at[0:last, :, chunks_of[k]], got_r.at[k])
-        own_r[k].wait()
-    for k, a, b in pairs_of(project(recv_r)):
-        big[k : k + BLOCK, :], big[DEPTHS + k : DEPTHS + k + BLOCK, :] = a, b
+        await_bytes(from_r.at[0, :, chunks_of[k]], sems_own.at[2 + NCH + k])
+    right[...] = stacked(recv_r)
 
     for kind in range(4):
         await_bytes(from_a.at[0:last], sent.at[kind])
@@ -446,33 +443,25 @@
 PARTS = 4
 
 
-def finish_kernel(R, update, first, cells, out, res, stage, sems):
+def finish_kernel(R, right, a3, first, cells, out, res, stage, sems):
     copies = [pltpu.make_async_copy(cells, res, sems.at[0])]
     copies[0].start()
-    block = 16
-
-    def shrink_second(i, carry):
-        top = pl.ds(pl.multiple_of(i * block, block), block)
-        low = pl.ds(pl.multiple_of(DEPTHS + i * block, block), block)
-        a, b = shrink_pair(
-            first[top, :] + STEP_SIZE * update[top, :], first[low, :] + STEP_SIZE * update[low, :]
+    rows = DEPTHS * R // PARTS
+    for k, a, b in pairs_of(mxu(a3[...], right[...])):
+        low = DEPTHS + k
+        pair = shrink_pair(
+            first[k : k + BLOCK, :] + STEP_SIZE * a, first[low : low + BLOCK, :] + STEP_SIZE * b
         )
-        for start, value in ((0, a), (DEPTHS, b)):
+        for start, value in zip((k, low), pair):
             for r in range(R):
-                stage[pl.ds((start + i * block) * R + r, block, stride=R), :] = value[
-                    :, r * LANES : (r + 1) * LANES
-                ]
-        return carry
-
-    steps = DEPTHS // block // PARTS
-    rows = DEPTHS * R // PARTS
-    for part in range(PARTS):
-        lax.fori_loop(part * steps, (part + 1) * steps, shrink_second, 0)
-        for half in range(2):
-            span = pl.ds(half * DEPTHS * R + part * rows, rows)
-            copy = pltpu.make_async_copy(stage.at[span], out.at[span], sems.at[1 + 2 * part + half])
-            copy.start()
-            copies.append(copy)
+                stage[pl.ds(start * R + r, BLOCK, stride=R), :] = value[:, r * LANES : (r + 1) * LANES]
+        part, rest = divmod(k + BLOCK, DEPTHS // PARTS)
+        if rest == 0:
+            for half in range(2):
+                span = pl.ds(half * DEPTHS * R + (part - 1) * rows, rows)
+                copy = pltpu.make_async_copy(stage.at[span], out.at[span], sems.at[2 * part - 1 + half])
+                copy.start()
+                copies.append(copy)
     for copy in copies:
         copy.wait()
 
@@ -497,15 +486,16 @@
     strip = pltpu.VMEM((SC * Y, LANES), F32)
     dma = pltpu.SemaphoreType.DMA
     args = (dirty.reshape(SC * Y, X), dirty.reshape(S, C, G, R, X), beams, chan_bins, pixel_order.reshape(Y, X))
-    update, first, cells = pl.pallas_call(
+    right, a3, first, cells = pl.pallas_call(
         functools.partial(kernel, d),
         out_shape=(
-            jax.ShapeDtypeStruct((2 * DEPTHS, N), F32),
+            jax.ShapeDtypeStruct((K3, N), BF16),
+            jax.ShapeDtypeStruct((2 * DEPTHS, K3), BF16),
             jax.ShapeDtypeStruct((2 * DEPTHS, N), F32),
             jax.ShapeDtypeStruct((SC * Y, X), F32),
         ),
         in_specs=[hbm, hbm, hbm, hbm, hbm],
-        out_specs=(vmem, vmem, vmem),
+        out_specs=(vmem, vmem, vmem, vmem),
         scratch_shapes=[
             pltpu.VMEM((SC * Y, X), F32),
             pltpu.VMEM(beams.shape, F32),
@@ -516,7 +506,6 @@
             pltpu.VMEM((C * 2 * len(hops(HALF)) * Y, 3 * LANES), BF16),
             pltpu.VMEM((KP, LANES), F32),
             pltpu.VMEM((K3, 2 * DEPTHS), F32),
-            pltpu.VMEM((2 * DEPTHS, K3), BF16),
             pltpu.VMEM((2 * KP, 2 * DEPTHS), BF16),
             pltpu.VMEM((2 * DEPTHS, N), BF16),
             pltpu.VMEM((2 * DEPTHS, N), BF16),
@@ -537,11 +526,11 @@
             jax.ShapeDtypeStruct((2 * DEPTHS * R, LANES), F32),
             jax.ShapeDtypeStruct((SC * Y, X), F32),
         ),
-        in_specs=[vmem, vmem, vmem],
+        in_specs=[vmem, vmem, vmem, vmem],
         out_specs=(hbm, hbm),
         scratch_shapes=[pltpu.VMEM((2 * DEPTHS * R + 8, LANES), F32), dma((1 + 2 * PARTS,))],
         compiler_params=pltpu.CompilerParams(vmem_limit_bytes=8 * 1024 * 1024),
-    )(update, first, cells)
+    )(right, a3, first, cells)
     return spectrum.reshape(2, DEPTHS, 1, N), residual.reshape(dirty.shape)
 
 

time: 19.4 us -> 19.1 us (0.985)
  Pallas kernels: 18.6 us -> 18.3 us
    pallas_call x1, Pallas kernels: 17.4 us -> 17.1 us  [on_device(): pl.pallas_call(functools.partial(kernel, d), out_shape=(jax.ShapeDtypeStr...]
where the time goes in v4:
time: 19.1 us; the launch traced here: 19 us
  Pallas kernels  18.3 us (96%)
  between operations  0.64 us (3%)
    pallas_call x1, Pallas kernels, on_device(): pl.pallas_call(functools.partial(kernel, d), out_shape=(jax.ShapeDtypeStr...  17.1 us
    pallas_call x1, Pallas kernels, on_device(): pl.pallas_call(functools.partial(finish_kernel, R), out_shape=(jax.ShapeD...  1.27 us

profile of v4, /device:TPU:0, one launch (start us, length us, event | category | flops | bytes accessed | tf_op | source)
XLA Modules:
  0.0 19.0 jit_solution(15641337994714955738)
XLA Ops:
  0.6 17.1 %shard_map.59 = (bf16[256,512]{1,0:T(8,128)(2,1)S(1)}, bf16[512,256]{1,0:T(8,128)(2,1)S(1)}, f32[512,512]{1,0:T(8,128)S(1)}, f32[288,128]{1,0:T(8,128)S(1)}) custom-call(f32[288,128]{1,0:T(8,128)} %bitcast.5, f32[2,9,4,4,128]{4,3,2,1,0:T(4,128)} %bitcast.6, f32[9,289]{1,0:T(8,128)} %beams_hbm.1, s32[36]{0:T(128)} %bins_hbm.1, s32[16,128]{1,0:T(8,128)} %bitcast.7), custom_call_target="tpu_custom_call" | custom-call | tf_op jit(solution)/shard_map/pallas_call | solution.py:489
  17.7 1.3 %shard_map.60 = (f32[2048,128]{1,0:T(8,128)}, f32[288,128]{1,0:T(8,128)}) custom-call(bf16[256,512]{1,0:T(8,128)(2,1)S(1)} %get-tuple-element.8.right, bf16[512,256]{1,0:T(8,128)(2,1)S(1)} %get-tuple-element.9.a3, f32[512,512]{1,0:T(8,128)S(1)} %get-tuple-element.10.first, f32[288,128]{1,0:T(8,128)S(1)} %get-tuple-element.11.cells), custom_call_target="tpu_custom_call" | custom-call | tf_op jit(solution)/shard_map/pallas_call | solution.py:523

commit v5 on v4

--- a/solution.py
+++ b/solution.py
@@ -195,11 +195,6 @@
             )
         return carry
 
-    lax.fori_loop(0, C, gather_dirty, 0)
-    for copy in own_copies(lambda p: to_d.at[:, :, p], lambda p: from_d.at[p], 1, got_d.at[0]):
-        copy.start()
-    own_d = pltpu.make_async_copy(to_d.at[:, :, g], from_d.at[g], sems_own.at[1])
-    own_d.start()
     bincol[...] = jnp.zeros_like(bincol)
     for q in range(G):
         for c in range(C):
@@ -360,6 +355,11 @@
             to_m.at[g, :, chunks_of[k]], rows.at[:, chunks_of[k], HALF // R + g], sems_own.at[2 + k]
         ).start()
 
+    lax.fori_loop(0, C, gather_dirty, 0)
+    for copy in own_copies(lambda p: to_d.at[:, :, p], lambda p: from_d.at[p], 1, got_d.at[0]):
+        copy.start()
+    own_d = pltpu.make_async_copy(to_d.at[:, :, g], from_d.at[g], sems_own.at[1])
+    own_d.start()
     lax.fori_loop(0, C, band, 0)
 
     lane = lax.broadcasted_iota(jnp.int32, (PY, LANES), 1)

time: 19.1 us -> 18.9 us (0.990)
  Pallas kernels: 18.3 us -> 18.1 us
    pallas_call x1, Pallas kernels: 17.1 us -> 16.8 us  [on_device(): pl.pallas_call(functools.partial(kernel, d), out_shape=(jax.ShapeDtypeStr...]
where the time goes in v5:
time: 18.9 us; the launch traced here: 18.7 us
  Pallas kernels  18.1 us (96%)
  between operations  0.64 us (3%)
    pallas_call x1, Pallas kernels, on_device(): pl.pallas_call(functools.partial(kernel, d), out_shape=(jax.ShapeDtypeStr...  16.8 us
    pallas_call x1, Pallas kernels, on_device(): pl.pallas_call(functools.partial(finish_kernel, R), out_shape=(jax.ShapeD...  1.27 us

profile of v5, /device:TPU:0, one launch (start us, length us, event | category | flops | bytes accessed | tf_op | source)
XLA Modules:
  0.0 18.7 jit_solution(18000636601946504305)
XLA Ops:
  0.6 16.8 %shard_map.59 = (bf16[256,512]{1,0:T(8,128)(2,1)S(1)}, bf16[512,256]{1,0:T(8,128)(2,1)S(1)}, f32[512,512]{1,0:T(8,128)S(1)}, f32[288,128]{1,0:T(8,128)S(1)}) custom-call(f32[288,128]{1,0:T(8,128)} %bitcast.5, f32[2,9,4,4,128]{4,3,2,1,0:T(4,128)} %bitcast.6, f32[9,289]{1,0:T(8,128)} %beams_hbm.1, s32[36]{0:T(128)} %bins_hbm.1, s32[16,128]{1,0:T(8,128)} %bitcast.7), custom_call_target="tpu_custom_call" | custom-call | tf_op jit(solution)/shard_map/pallas_call | solution.py:489
  17.4 1.3 %shard_map.60 = (f32[2048,128]{1,0:T(8,128)}, f32[288,128]{1,0:T(8,128)}) custom-call(bf16[256,512]{1,0:T(8,128)(2,1)S(1)} %get-tuple-element.8.right, bf16[512,256]{1,0:T(8,128)(2,1)S(1)} %get-tuple-element.9.a3, f32[512,512]{1,0:T(8,128)S(1)} %get-tuple-element.10.first, f32[288,128]{1,0:T(8,128)S(1)} %get-tuple-element.11.cells), custom_call_target="tpu_custom_call" | custom-call | tf_op jit(solution)/shard_map/pallas_call | solution.py:523

commit v6 on v5

--- a/solution.py
+++ b/solution.py
@@ -91,7 +91,6 @@
     got_h,
     got_r,
     sems_in,
-    sems_own,
     joined,
 ):
     G, T, R, Y, C, S, CC, NCH, HALF, BEAM = (
@@ -114,7 +113,7 @@
     to_d, to_r = (ref.reshape(S, C, G, R, X) for ref in (slots_d, slots_r))
     to_m = send_m.reshape(G, S, C, R, X)
     rows = padded.reshape(S, C, PY // R, R, X)
-    own_a = pltpu.make_async_copy(blocks_hbm.at[:, :, g], from_a.at[g], sems_own.at[0])
+    own_a = pltpu.make_async_copy(blocks_hbm.at[:, :, g], from_a.at[g], got_a.at[0])
     for load in loads:
         load.start()
     own_a.start()
@@ -302,8 +301,7 @@
         for p in range(last):
             pl.semaphore_signal(joined, inc=1, device_id=(p, t), device_id_type=MESH)
 
-    await_bytes(from_a.at[0:last], got_a.at[0])
-    own_a.wait()
+    await_bytes(from_a, got_a.at[0])
     for k, a, b in pairs_of(project(recv_a)):
         a, b = shrink_pair(a, b)
         first_hi[k : k + BLOCK, :], first_lo[k : k + BLOCK, :] = split(a)
@@ -352,14 +350,13 @@
         ):
             copy.start()
         pltpu.make_async_copy(
-            to_m.at[g, :, chunks_of[k]], rows.at[:, chunks_of[k], HALF // R + g], sems_own.at[2 + k]
+            to_m.at[g, :, chunks_of[k]], rows.at[:, chunks_of[k], HALF // R + g], got_m.at[k]
         ).start()
 
     lax.fori_loop(0, C, gather_dirty, 0)
     for copy in own_copies(lambda p: to_d.at[:, :, p], lambda p: from_d.at[p], 1, got_d.at[0]):
         copy.start()
-    own_d = pltpu.make_async_copy(to_d.at[:, :, g], from_d.at[g], sems_own.at[1])
-    own_d.start()
+    pltpu.make_async_copy(to_d.at[:, :, g], from_d.at[g], got_d.at[0]).start()
     lax.fori_loop(0, C, band, 0)
 
     lane = lax.broadcasted_iota(jnp.int32, (PY, LANES), 1)
@@ -403,8 +400,7 @@
 
     def chunk(k, carry):
         channels = pl.ds(k * CC, CC)
-        await_bytes(to_m.at[0:last, :, 0:CC], got_m.at[k])
-        await_bytes(to_m.at[0, :, 0:CC], sems_own.at[2 + k])
+        await_bytes(to_m.at[:, :, 0:CC], got_m.at[k])
         await_halo(1, k, has_next)
         await_halo(0, k, has_prev)
         for c in range(CC):
@@ -416,20 +412,18 @@
         ):
             copy.start()
         pltpu.make_async_copy(
-            to_r.at[:, channels, g], from_r.at[g, :, channels], sems_own.at[2 + NCH + k]
+            to_r.at[:, channels, g], from_r.at[g, :, channels], got_r.at[k]
         ).start()
         return carry
 
     lax.fori_loop(0, NCH, chunk, 0)
 
-    await_bytes(from_d.at[0:last], got_d.at[0])
-    own_d.wait()
+    await_bytes(from_d, got_d.at[0])
     for k, a, b in pairs_of(project(recv_d)):
         first_slots[k : k + BLOCK, :], first_slots[DEPTHS + k : DEPTHS + k + BLOCK, :] = shrink_pair(a, b)
 
     for k in range(NCH):
-        await_bytes(from_r.at[0:last, :, chunks_of[k]], got_r.at[k])
-        await_bytes(from_r.at[0, :, chunks_of[k]], sems_own.at[2 + NCH + k])
+        await_bytes(from_r.at[:, :, chunks_of[k]], got_r.at[k])
     right[...] = stacked(recv_r)
 
     for kind in range(4):
@@ -514,7 +508,7 @@
             strip,
         ]
         + [share] * 4
-        + [dma((5,)), dma((1,)), dma((1,)), dma((NCH,)), dma((2, NCH)), dma((NCH,)), dma((4,)), dma((2 + 2 * NCH,))]
+        + [dma((5,)), dma((1,)), dma((1,)), dma((NCH,)), dma((2, NCH)), dma((NCH,)), dma((4,))]
         + [pltpu.SemaphoreType.REGULAR],
         compiler_params=pltpu.CompilerParams(
             collective_id=0, has_side_effects=True, vmem_limit_bytes=40 * 1024 * 1024

time: 18.9 us -> 18.8 us (level)
  no operation moved by 1% of the time
where the time goes in v6:
time: 18.8 us; the launch traced here: 18.6 us
  Pallas kernels  18 us (96%)
  between operations  0.64 us (3%)
    pallas_call x1, Pallas kernels, on_device(): pl.pallas_call(functools.partial(kernel, d), out_shape=(jax.ShapeDtypeStr...  16.7 us
    pallas_call x1, Pallas kernels, on_device(): pl.pallas_call(functools.partial(finish_kernel, R), out_shape=(jax.ShapeD...  1.26 us

profile of v6, /device:TPU:0, one launch (start us, length us, event | category | flops | bytes accessed | tf_op | source)
XLA Modules:
  0.0 18.6 jit_solution(6652036528990777296)
XLA Ops:
  0.6 16.7 %shard_map.59 = (bf16[256,512]{1,0:T(8,128)(2,1)S(1)}, bf16[512,256]{1,0:T(8,128)(2,1)S(1)}, f32[512,512]{1,0:T(8,128)S(1)}, f32[288,128]{1,0:T(8,128)S(1)}) custom-call(f32[288,128]{1,0:T(8,128)} %bitcast.5, f32[2,9,4,4,128]{4,3,2,1,0:T(4,128)} %bitcast.6, f32[9,289]{1,0:T(8,128)} %beams_hbm.1, s32[36]{0:T(128)} %bins_hbm.1, s32[16,128]{1,0:T(8,128)} %bitcast.7), custom_call_target="tpu_custom_call" | custom-call | tf_op jit(solution)/shard_map/pallas_call | solution.py:483
  17.4 1.3 %shard_map.60 = (f32[2048,128]{1,0:T(8,128)}, f32[288,128]{1,0:T(8,128)}) custom-call(bf16[256,512]{1,0:T(8,128)(2,1)S(1)} %get-tuple-element.8.right, bf16[512,256]{1,0:T(8,128)(2,1)S(1)} %get-tuple-element.9.a3, f32[512,512]{1,0:T(8,128)S(1)} %get-tuple-element.10.first, f32[288,128]{1,0:T(8,128)S(1)} %get-tuple-element.11.cells), custom_call_target="tpu_custom_call" | custom-call | tf_op jit(solution)/shard_map/pallas_call | solution.py:517
